TPU v7x, 32 devices: a whole 2x2x4 slice. The times are simulated.
32 devices in a mesh: cells: 8 (over y, x, core), obs: 4 (over z).
Axes of the slice: x: 2, y: 2, z: 4, core: 2. Of those that a mesh axis runs over, the one named last changes fastest.
Arguments:
- histories: bfloat16 [64, 384], P('obs'), may hold values from -6 to 6
- amplitude: bfloat16 [64, 5, 8192], P('obs', None, 'cells'), may hold values from -0.75 to 0.75
- weights: bfloat16 [8192, 256], P('cells'), may hold values from -0.375 to 0.375
- retarded: int32 [64, 64], P('obs', 'cells'), may hold values from 0 to 128
- owner_block: int32 [8192], P('cells'), may hold values from 0 to 7, as said below
- owner_cell: int32 [8192], P('cells'), may hold values from 0 to 16383
- adjoint: float32 [5, 16, 64, 128], P(None, 'cells', 'obs'), may hold values from -6 to 6
- step_size: float32 [16, 64, 128], P('cells', 'obs'), may hold values from 0.1 to 0.6
- jacobian: float32 [8, 3, 5, 5], P('cells'), may hold values from -6 to 6
Outputs:
- adjoint_next: float32 [5, 16, 64, 128], P(None, 'cells', 'obs')
- panel_source: float32 [5, 8192], P(None, 'cells')
Inputs may be any that keep to these rules, and one draw needn't show every extreme that they name: `owner_block`: among each device's 1024 panels at most 512 name one owner block; one owner block, drawn from the seed, is named by exactly 512 panels of every device.
All inputs are finite; a program needn't handle non-finite values.
Results may differ from a plain program's by a relative error of at most 0.0003.
Values sent between devices are 32-bit elements; how exact they have to be, the bound alone decides.
A program may use at most 192 MiB of HBM per device.

v0:
```python
import jax
import jax.numpy as jnp
from jax import lax
from jax.sharding import PartitionSpec as P

SAMPLES = 256
SPAN = 128
COMP = 5
TILE = 128


smoothing = 0.25


def extended(cells, sides, width, closed):
    for axis, dim in sides:
        count = lax.axis_size(axis)
        ends = count if closed else count - 1
        head = lax.slice_in_dim(cells, 0, width, axis=dim)
        tail = lax.slice_in_dim(cells, cells.shape[dim] - width, cells.shape[dim], axis=dim)
        cells = jnp.concatenate(
            [
                lax.ppermute(tail, axis, [(i, (i + 1) % count) for i in range(ends)]),
                cells,
                lax.ppermute(head, axis, [((i + 1) % count, i) for i in range(ends)]),
            ],
            axis=dim,
        )
    return cells


def on_device(
    histories, amplitude, weights, retarded, owner_block, owner_cell, adjoint, step_size, jacobian
):
    tile_count = weights.shape[0] // TILE
    weights_tiled = weights.reshape(tile_count, TILE, SAMPLES)
    observers_local = histories.shape[0]
    history_len = histories.shape[1]
    shifted = jnp.broadcast_to(histories[:, None, :], (observers_local, tile_count, history_len))
    for bit_number in range(SPAN.bit_length()):
        amount = 1 << bit_number
        moved = jnp.concatenate(
            [
                shifted[..., amount:],
                jnp.zeros((observers_local, tile_count, amount), shifted.dtype),
            ],
            axis=2,
        )
        chosen = retarded >> bit_number & 1 == 1
        shifted = jnp.where(chosen[:, :, None], moved, shifted)
    window = shifted[..., :SAMPLES]
    projected = jnp.einsum(
        "tps,ots->otp", weights_tiled, window, preferred_element_type=jnp.float32
    )
    projected = projected.reshape(projected.shape[0], -1)
    partial_value = jnp.sum(amplitude.astype(jnp.float32) * projected[:, None, :], axis=0)
    panel_source = lax.psum(partial_value, "obs")
    my_block = lax.axis_index("cells")
    my_group = lax.axis_index("obs")
    azimuth_local = adjoint.shape[1]
    radial_local = adjoint.shape[2]
    axial_len = adjoint.shape[3]
    radial_all = radial_local * lax.axis_size("obs")
    block_cells = azimuth_local * radial_all * axial_len
    device_cells = azimuth_local * radial_local * axial_len
    target = (owner_block * block_cells + owner_cell).reshape(1, -1)
    empty_field = jnp.zeros((COMP, device_cells), jnp.float32)
    devices = lax.axis_size("cells")
    capacity = 4 * owner_block.shape[0] // devices
    one_hot = (owner_block[:, None] == jnp.arange(devices, dtype=jnp.int32)[None, :]).astype(
        jnp.int32
    )
    slot_rank = jnp.sum(jnp.cumsum(one_hot, axis=0) * one_hot, axis=1) - 1
    slot_of = owner_block * capacity + slot_rank
    outgoing = jnp.zeros((COMP, devices * capacity), jnp.float32).at[:, slot_of].set(panel_source)
    out_index = jnp.full((1, devices * capacity), -1, jnp.int32).at[0, slot_of].set(target[0])
    received, arrivals = (
        lax.all_to_all(outgoing, "cells", split_axis=1, concat_axis=1, tiled=True),
        lax.all_to_all(out_index, "cells", split_axis=1, concat_axis=1, tiled=True),
    )
    flat_index = arrivals[0]
    block_of = flat_index // block_cells
    within = flat_index % block_cells
    azimuth = within // (radial_all * axial_len)
    radius = within // axial_len % radial_all
    axial = within % axial_len
    is_mine = (block_of == my_block) & (radius // radial_local == my_group) & (flat_index >= 0)
    position = (azimuth * radial_local + radius - my_group * radial_local) * axial_len + axial
    landing = jnp.where(is_mine, position, device_cells)
    surface = empty_field.at[:, landing].add(received, mode="drop")
    widened = extended(adjoint, (("cells", 1),), 1, True)
    heightened = extended(adjoint, (("obs", 2),), 1, False)
    deepened = jnp.pad(adjoint, ((0, 0), (0, 0), (0, 0), (1, 1)))
    matrices = jacobian[0]
    neighbours = (
        (widened[:, 2:], widened[:, :-2]),
        (heightened[:, :, 2:], heightened[:, :, :-2]),
        (deepened[..., 2:], deepened[..., :-2]),
    )
    summed = jnp.zeros_like(adjoint)
    for direction in range(3):
        forward, backward = neighbours[direction]
        rotated = jnp.einsum(
            "kc,karz->carz",
            matrices[direction],
            forward - backward,
            precision=lax.Precision.HIGHEST,
        )
        summed = summed + (0.5 * rotated + smoothing * (forward - 2.0 * adjoint + backward))
    adjoint_next = adjoint + step_size[None] * summed + surface.reshape(adjoint.shape)
    return (adjoint_next, panel_source)


def solution(mesh):
    return jax.shard_map(
        on_device,
        mesh=mesh,
        in_specs=(
            P("obs", None),
            P("obs", None, "cells"),
            P("cells", None),
            P("obs", "cells"),
            P("cells"),
            P("cells"),
            P(None, "cells", "obs", None),
            P("cells", "obs", None),
            P("cells", None, None, None),
        ),
        out_specs=(P(None, "cells", "obs", None), P(None, "cells")),
        check_vma=False,
    )
```

profile of v0, /device:TPU:0, one launch (start us, length us, event | category | flops | bytes accessed | tf_op | source)
XLA Modules:
  0.0 93.0 jit_solution(10608358137834040790)
XLA Ops:
  0.6 0.8 fusion.22
  1.4 2.3 %reduce-window.6 = s32[8,8,128]{2,1,0:T(8,128)S(1)} reduce-window(s32[8,8,128]{2,1,0:T(8,128)S(1)} %fusion.22, s32[]{:T(128)} %constant.118.clone.1), window={size=1x1x128 pad=0_0x0_0x127_0}, to_apply=%region_0.1 | reduce-window | flops 1040384 | bytes 65540 | tf_op jit(solution)/shard_map/reduce-window
  3.6 0.3 slice_reduce_fusion
  4.2 0.7 fusion.21
  4.9 0.7 multiply_add_fusion
  5.6 0.7 fusion.25
  6.3 0.7 and_reduce_fusion
  7.1 4.9 %scatter_custom_fusion.2 = s32[4096]{0:T(1024)} fusion(s32[1024]{0:T(1024)S(1)} %broadcast_select_fusion, s32[1024]{0:T(1024)S(1)} %get-tuple-element.25, s32[]{:T(128)} %constant.116.clone.1), kind=kCustom, calls=%fused_computation.79 | custom fusion | bytes 16388
  12.0 5.2 %all-to-all-start = ((s32[1,8,512]{2,0,1:T(1,128)}), s32[1,8,512]{2,0,1:T(1,128)S(1)}, u32[]{:S(2)}, u32[]{:S(2)}) async-start(s32[1,8,512]{2,0,1:T(1,128)} %bitcast.12), calls=%async_computation | async-start | bytes 32768 | tf_op jit(solution)/shard_map/all_to_all | solution.py:79
  17.2 0.9 %copy.91 = f32[5,2,16,128]{3,0,2,1:T(8,128)S(1)} copy(f32[5,2,16,128]{3,2,1,0:T(8,128)} %param.15) | data formatting | bytes 163840 | tf_op args[6]
  18.1 1.3 %collective-permute-start.2 = (f32[5,2,1,128]{3,0,2,1:T(8,128)S(1)}, f32[5,2,1,128]{3,0,2,1:T(8,128)}, u32[]{:S(2)}, u32[]{:S(2)}) collective-permute-start(f32[5,2,1,128]{3,0,2,1:T(8,128)S(1)} %get-tuple-element.13), channel_id=1, source_target_pairs={{1,0},{2,1},{3,2},{5,4},{6,5},{7,6},{9,8},{10,9},{11,10},{13,12},{... | collective-permute-start | bytes 15368 | tf_op jit(solution)/shard_map/ppermute | solution.py:25
  19.4 5.1 %collective-permute-start.3 = (f32[5,2,1,128]{3,0,2,1:T(8,128)S(1)}, f32[5,2,1,128]{3,0,2,1:T(8,128)}, u32[]{:S(2)}, u32[]{:S(2)}) collective-permute-start(f32[5,2,1,128]{3,0,2,1:T(8,128)S(1)} %get-tuple-element.12), channel_id=1, source_target_pairs={{0,1},{1,2},{2,3},{4,5},{5,6},{6,7},{8,9},{9,10},{10,11},{12,13},{... | collective-permute-start | bytes 15368 | tf_op jit(solution)/shard_map/ppermute | solution.py:23
  24.6 0.6 fusion.32
  25.2 2.1 %collective-permute-start = (f32[5,1,16,128]{3,0,2,1:T(8,128)}, f32[5,1,16,128]{3,0,2,1:T(8,128)S(1)}, u32[]{:S(2)}, u32[]{:S(2)}) collective-permute-start(f32[5,1,16,128]{3,0,2,1:T(8,128)} %get-tuple-element.11), channel_id=1, source_target_pairs={{4,0},{8,4},{12,8},{16,12},{20,16},{24,20},{28,24},{0,28},{5,1},{9... | collective-permute-start | bytes 122888 | tf_op jit(solution)/shard_map/ppermute | solution.py:25
  27.3 0.7 and_compare_fusion.7
  28.0 0.8 slice.95
  28.8 0.8 pad_select_fusion.6
  29.7 0.9 pad_select_fusion.5
  30.7 0.8 pad_select_fusion.4
  32.7 1.1 %fusion.10 = f32[5,2,16,128]{3,0,2,1:T(8,128)} fusion(f32[5,2,16,128]{3,0,2,1:T(8,128)S(1)} %copy.91, f32[1,1,5,5]{3,0,2,1:T(1,128)S(1)} %get-tuple-element.16), kind=kOutput, calls=%fused_computation.16 | convolution fusion | flops 1372160 | bytes 346624 | tf_op jit(solution)/shard_map/kc,karz->carz/dot_general | solution.py:103
  33.8 17.3 %psum.7 = f32[5,1024]{1,0:T(8,128)S(1)} all-reduce(f32[5,1024]{1,0:T(8,128)S(1)} %multiply_reduce_fusion), channel_id=1, replica_groups=mesh['cells'=8,'obs'=4] {'obs'}, use_global_device_ids=true, to_apply=%region_5.6 | all-reduce | flops 5120 | bytes 40960 | tf_op jit(solution)/shard_map/psum | solution.py:57
  51.4 3.6 %scatter_custom_fusion = f32[5,4096]{0,1:T(8,128)S(1)} fusion(s32[1024]{0:T(1024)S(1)} %get-tuple-element.26, f32[1024,5]{1,0:T(8,128)S(1)} %copy.93, f32[]{:T(128)} %constant.115.clone.1), kind=kCustom, calls=%fused_computation.20 | custom fusion | bytes 81924 | tf_op jit(solution)/shard_map/scatter | solution.py:75
  55.0 1.3 %copy.94 = f32[5,8,512]{2,0,1:T(8,128)} copy(f32[5,8,512]{0,2,1:T(8,128)S(1)} %bitcast.73) | data formatting | bytes 163840 | tf_op jit(solution)/shard_map/all_to_all | solution.py:78
  56.3 1.1 %fusion.9 = f32[5,2,16,128]{3,0,2,1:T(8,128)S(1)} fusion(f32[5,2,1,128]{3,0,2,1:T(8,128)} %collective-permute-done.2, f32[5,2,16,128]{3,0,2,1:T(8,128)S(1)} %copy.91, f32[5,2,1,128]{3,0,2,1:T(8,128)} %collective-permute-done.3, f32[1,1,5,5]{3,0,2,1:T(1,128)S(1)} %get-tuple-element.15), kind=kOutput, calls=%fused_computation.15 | convolution fusion | flops 1454080 | bytes 174180 | tf_op jit(solution)/shard_map/kc,karz->carz/dot_general | solution.py:103
  57.4 3.4 %all-to-all-start.1 = ((f32[5,8,512]{2,0,1:T(8,128)}), f32[5,8,512]{2,0,1:T(8,128)S(1)}, u32[]{:S(2)}, u32[]{:S(2)}) async-start(f32[5,8,512]{2,0,1:T(8,128)} %copy.94), calls=%async_computation.1 | async-start | bytes 262144 | tf_op jit(solution)/shard_map/all_to_all | solution.py:78
  60.8 0.5 compare_select_fusion
  61.3 5.0 %all-to-all-done.1 = f32[5,8,512]{2,0,1:T(8,128)S(1)} async-done(((f32[5,8,512]{2,0,1:T(8,128)}), f32[5,8,512]{2,0,1:T(8,128)S(1)}, u32[]{:S(2)}, u32[]{:S(2)}) %all-to-all-start.1) | async-done | bytes 81952 | tf_op jit(solution)/shard_map/all_to_all | solution.py:78
  66.2 2.0 %copy.95 = f32[4096,5]{1,0:T(8,128)} copy(f32[4096,5]{0,1:T(8,128)S(1)} %bitcast.74) | data formatting | bytes 163840 | tf_op jit(solution)/shard_map/all_to_all | solution.py:78
  68.2 23.2 %scatter_custom_fusion.1 = f32[5,4096]{0,1:T(8,128)S(1)} fusion(s32[4096]{0:T(1024)S(1)} %bitcast.82, f32[4096,5]{1,0:T(8,128)} %copy.95, f32[]{:T(128)} %constant.115.clone.1), kind=kCustom, calls=%fused_computation.18 | custom fusion | flops 20480 | bytes 82432 | tf_op jit(solution)/shard_map/scatter-add | solution.py:90
  91.4 0.6 copy.97
  92.0 0.3 fusion.8
  92.4 0.7 copy.98
  (39 shorter events, 1.8 us)
Async XLA Ops:
  0.6 31.7 %copy-start = (bf16[1024,256]{1,0:T(8,128)(2,1)S(1)}, bf16[1024,256]{1,0:T(8,128)(2,1)}, u32[]{:S(2)}) copy-start(bf16[1024,256]{1,0:T(8,128)(2,1)} %param.11) | copy-start | bytes 1572868
  12.0 45.4 %all-to-all-start = ((s32[1,8,512]{2,0,1:T(1,128)}), s32[1,8,512]{2,0,1:T(1,128)S(1)}, u32[]{:S(2)}, u32[]{:S(2)}) async-start(s32[1,8,512]{2,0,1:T(1,128)} %bitcast.12), calls=%async_computation | async-start | bytes 32768 | tf_op jit(solution)/shard_map/all_to_all | solution.py:79
  18.1 38.1 %collective-permute-start.2 = (f32[5,2,1,128]{3,0,2,1:T(8,128)S(1)}, f32[5,2,1,128]{3,0,2,1:T(8,128)}, u32[]{:S(2)}, u32[]{:S(2)}) collective-permute-start(f32[5,2,1,128]{3,0,2,1:T(8,128)S(1)} %get-tuple-element.13), channel_id=1, source_target_pairs={{1,0},{2,1},{3,2},{5,4},{6,5},{7,6},{9,8},{10,9},{11,10},{13,12},{... | collective-permute-start | bytes 15368 | tf_op jit(solution)/shard_map/ppermute | solution.py:25
  19.4 36.9 %collective-permute-start.3 = (f32[5,2,1,128]{3,0,2,1:T(8,128)S(1)}, f32[5,2,1,128]{3,0,2,1:T(8,128)}, u32[]{:S(2)}, u32[]{:S(2)}) collective-permute-start(f32[5,2,1,128]{3,0,2,1:T(8,128)S(1)} %get-tuple-element.12), channel_id=1, source_target_pairs={{0,1},{1,2},{2,3},{4,5},{5,6},{6,7},{8,9},{9,10},{10,11},{12,13},{... | collective-permute-start | bytes 15368 | tf_op jit(solution)/shard_map/ppermute | solution.py:23
  25.2 66.8 %collective-permute-start = (f32[5,1,16,128]{3,0,2,1:T(8,128)}, f32[5,1,16,128]{3,0,2,1:T(8,128)S(1)}, u32[]{:S(2)}, u32[]{:S(2)}) collective-permute-start(f32[5,1,16,128]{3,0,2,1:T(8,128)} %get-tuple-element.11), channel_id=1, source_target_pairs={{4,0},{8,4},{12,8},{16,12},{20,16},{24,20},{28,24},{0,28},{5,1},{9... | collective-permute-start | bytes 122888 | tf_op jit(solution)/shard_map/ppermute | solution.py:25
  27.3 64.7 %collective-permute-start.1 = (f32[5,1,16,128]{3,0,2,1:T(8,128)S(1)}, f32[5,1,16,128]{3,0,2,1:T(8,128)S(1)}, u32[]{:S(2)}, u32[]{:S(2)}) collective-permute-start(f32[5,1,16,128]{3,0,2,1:T(8,128)S(1)} %get-tuple-element.10), channel_id=1, source_target_pairs={{0,4},{4,8},{8,12},{12,16},{16,20},{20,24},{24,28},{28,0},{1,5},{5... | collective-permute-start | bytes 122888 | tf_op jit(solution)/shard_map/ppermute | solution.py:23
  28.8 3.9 %copy-start.5 = (f32[1,3,5,5]{3,0,2,1:T(1,128)S(1)}, f32[1,3,5,5]{3,0,2,1:T(1,128)}, u32[]{:S(2)}) copy-start(f32[1,3,5,5]{3,0,2,1:T(1,128)} %param.17) | copy-start | bytes 904
  29.7 4.0 %copy-start.1 = (bf16[16,5,1024]{2,0,1:T(8,128)(2,1)S(1)}, bf16[16,5,1024]{2,0,1:T(8,128)(2,1)}, u32[]{:S(2)}) copy-start(bf16[16,5,1024]{2,0,1:T(8,128)(2,1)} %param.10) | copy-start | bytes 491524
  51.2 5.1 %copy-start.2 = (f32[5,1024]{1,0:T(8,128)}, f32[5,1024]{1,0:T(8,128)S(1)}, u32[]{:S(2)}) copy-start(f32[5,1024]{1,0:T(8,128)S(1)} %psum.7) | copy-start | bytes 61444
  57.4 8.8 %all-to-all-start.1 = ((f32[5,8,512]{2,0,1:T(8,128)}), f32[5,8,512]{2,0,1:T(8,128)S(1)}, u32[]{:S(2)}, u32[]{:S(2)}) async-start(f32[5,8,512]{2,0,1:T(8,128)} %copy.94), calls=%async_computation.1 | async-start | bytes 262144 | tf_op jit(solution)/shard_map/all_to_all | solution.py:78
  68.2 23.8 %copy-start.3 = (f32[5,2,16,128]{3,0,2,1:T(8,128)S(1)}, f32[5,2,16,128]{3,0,2,1:T(8,128)}, u32[]{:S(2)}) copy-start(f32[5,2,16,128]{3,0,2,1:T(8,128)} %fusion.10) | copy-start | bytes 245764
  68.2 23.8 %copy-start.4 = (f32[2,16,128]{2,1,0:T(8,128)S(1)}, f32[2,16,128]{2,1,0:T(8,128)}, u32[]{:S(2)}) copy-start(f32[2,16,128]{2,1,0:T(8,128)} %param.16) | copy-start | bytes 49156
where the time goes:
time: 94.1 us; the launch traced here: 93 us
  other arithmetic  33.4 us (35%)
  blocking collectives  17.3 us (18%)
  starting transfers between devices  17.1 us (18%)
  local copies, waits for them, and re-layouts  16.5 us (18%)
  waiting for transfers between devices  4.98 us (5%)
  matrix products  2.79 us (3%)
    scatter-add x1, other arithmetic, on_device(): surface = empty_field.at[:, landing].add(received, mode='drop')  23.2 us
    psum x1, blocking collectives, on_device(): panel_source = lax.psum(partial_value, 'obs')  17.3 us
    unnamed x15, local copies, waits for them, and re-layouts  6.53 us
    all_to_all x1, starting transfers between devices, on_device(): lax.all_to_all(out_index, 'cells', split_axis=1, concat_axis=1, tiled=True)  5.2 us
    ppermute x2, starting transfers between devices, extended(): lax.ppermute(tail, axis, [(i, (i + 1) % count) for i in range(ends)])  5.15 us
    all_to_all x1, waiting for transfers between devices, on_device(): lax.all_to_all(outgoing, 'cells', split_axis=1, concat_axis=1, tiled=True)  4.97 us
    scatter x1, local copies, waits for them, and re-layouts, on_device(): jnp.zeros((COMP, devices * capacity), jnp.float32).at[:, slot_of]  3.59 us
    all_to_all x1, starting transfers between devices, on_device(): lax.all_to_all(outgoing, 'cells', split_axis=1, concat_axis=1, tiled=True)  3.38 us
  transfers between devices with their start and end apart: 6, of which 1 were waited for; matrix products, arithmetic and copies ran while one was open for 43% of the time, Pallas kernels for 0%

commit v1 on v0

v1 whole, which is shorter than its diff:
```python
import functools

import jax
import jax.numpy as jnp
from jax import lax
from jax.experimental import pallas as pl
from jax.experimental.pallas import tpu as pltpu
from jax.sharding import PartitionSpec as P

MESH = pl.DeviceIdType.MESH
SMOOTHING = 0.25
NT = (((1,), (1,)), ((), ()))


def div(x, d):
    if d & (d - 1) == 0:
        return lax.shift_right_logical(x, jnp.full_like(x, d.bit_length() - 1))
    return lax.div(x, jnp.full_like(x, d))


def mod(x, d):
    if d & (d - 1) == 0:
        return x & (d - 1)
    return lax.rem(x, jnp.full_like(x, d))


def partner(me, j, n):
    if n & (n - 1):
        return lax.rem(me + j, n)
    out = me
    for k in range(n.bit_length() - 1):
        if j >> k & 1:
            out = out + (1 - 2 * ((me // (1 << k)) % 2)) * (1 << k)
    return out


def kernel(
    nc, no,
    hist_h, amp_h, wts_h, ret_h, ob_h, oc_h, adj_h, step_h, jac_h,
    out_ref, ps_ref,
    hist, amp, wts, ret, ob, oc, adj, step, jac,
    part, src, tgt, halo_a, halo_r, a_buf, bt, acc,
    in_sem, ps_send, ps_recv, s_send, s_recv, t_send, t_recv, h_send, h_recv,
):
    me, g = lax.axis_index("cells"), lax.axis_index("obs")
    loads = [
        pltpu.make_async_copy(h, v, in_sem.at[i])
        for i, (h, v) in enumerate(
            [(hist_h, hist), (ret_h, ret), (ob_h, ob), (oc_h, oc), (wts_h, wts), (amp_h, amp),
             (adj_h, adj), (step_h, step), (jac_h, jac)]
        )
    ]
    for c in loads:
        c.start()
    barrier = pltpu.get_barrier_semaphore()
    peers_c = [partner(me, j, nc) for j in range(nc)]
    peers_o = [lax.rem(g + k, no) for k in range(no)]
    for j in range(1, nc):
        pl.semaphore_signal(barrier, inc=1, device_id=(peers_c[j], g), device_id_type=MESH)
    for k in range(1, no):
        pl.semaphore_signal(barrier, inc=1, device_id=(me, peers_o[k]), device_id_type=MESH)

    nobs, comp = amp.shape[0], amp.shape[1]
    samples = wts.shape[1]
    hlen = hist.shape[1]
    tiles = ret.shape[1]
    tile = wts.shape[0] // tiles
    az, rl, nz = adj.shape[1:]
    radial_all = rl * no
    block_cells = az * radial_all * nz

    loads[0].wait()
    loads[1].wait()
    loads[2].wait()
    loads[3].wait()
    tgt[0] = ob[...] * block_cells + oc[...]
    series = hist[...].astype(jnp.float32)
    offsets = ret[...]
    span = hlen - samples
    windows = []
    for t in range(tiles):
        off = offsets[:, t : t + 1]
        x = series
        for bit in reversed(range(span.bit_length())):
            amount = 1 << bit
            moved = pltpu.roll(x, hlen - amount, 1)
            x = jnp.where((off >> bit & 1) == 1, moved, x)
        windows.append(x[:, :samples].astype(jnp.bfloat16))
    loads[4].wait()
    loads[5].wait()
    for t in range(tiles):
        cols = slice(t * tile, (t + 1) * tile)
        proj = lax.dot_general(windows[t], wts[cols, :], NT, preferred_element_type=jnp.float32)
        total = jnp.zeros((comp, tile), jnp.float32)
        for o in range(nobs):
            total = total + amp[o, :, cols].astype(jnp.float32) * proj[o : o + 1, :]
        for c in range(comp):
            part[g, c, t : t + 1, :] = total[c : c + 1, :]
    loads[6].wait()
    loads[7].wait()
    loads[8].wait()

    pl.semaphore_wait(barrier, nc - 1 + no - 1)

    def remote(s, d, ss, rs, dev):
        return pltpu.make_async_remote_copy(
            src_ref=s, dst_ref=d, send_sem=ss, recv_sem=rs, device_id=dev, device_id_type=MESH
        )

    part_copies = [
        remote(part.at[g], part.at[g], ps_send.at[k], ps_recv.at[k], (me, peers_o[k]))
        for k in range(1, no)
    ]
    for c in part_copies:
        c.start()
    tgt_copies = [
        remote(tgt.at[0], tgt.at[j], t_send.at[j], t_recv.at[j], (peers_c[j], g))
        for j in range(1, nc)
    ]
    for c in tgt_copies:
        c.start()
    after, before = lax.rem(me + 1, nc), lax.rem(me + nc - 1, nc)
    az_copies = [
        remote(adj.at[:, az - 1], halo_a.at[0], h_send.at[0], h_recv.at[0], (after, g)),
        remote(adj.at[:, 0], halo_a.at[1], h_send.at[1], h_recv.at[1], (before, g)),
    ]
    for c in az_copies:
        c.start()
    g_after, g_before = lax.rem(g + 1, no), lax.rem(g + no - 1, no)
    up = remote(adj.at[:, :, pl.ds(rl - 8, 8)], halo_r.at[0], h_send.at[2], h_recv.at[2], (me, g_after))
    down = remote(adj.at[:, :, pl.ds(0, 8)], halo_r.at[1], h_send.at[3], h_recv.at[3], (me, g_before))
    has_after, has_before = g < no - 1, g > 0

    @pl.when(has_after)
    def _():
        up.start()

    @pl.when(has_before)
    def _():
        down.start()

    column_id = lax.broadcasted_iota(jnp.int32, (az * nz, tile), 0) + me * (az * nz)
    row_id = lax.broadcasted_iota(jnp.int32, (rl, tile), 0) + g * rl

    def build_columns(j, slot):
        flat = tgt[j]
        code = div(flat, radial_all * nz) * nz + mod(flat, nz)
        for t in range(tiles):
            hit = code[t : t + 1, :] == column_id
            bt[slot, :, t * tile : (t + 1) * tile] = jnp.where(hit, 1.0, 0.0).astype(jnp.bfloat16)

    few = bt.shape[0] == nc
    if few:
        build_columns(0, 0)

    for c in az_copies:
        c.wait_recv()

    @pl.when(has_before)
    def _():
        up.wait_recv()

    @pl.when(has_after)
    def _():
        down.wait_recv()

    @pl.when(jnp.logical_not(has_before))
    def _():
        halo_r[0] = jnp.zeros(halo_r.shape[1:], jnp.float32)

    @pl.when(jnp.logical_not(has_after))
    def _():
        halo_r[1] = jnp.zeros(halo_r.shape[1:], jnp.float32)

    row = lax.broadcasted_iota(jnp.int32, (rl, nz), 0)
    lane = lax.broadcasted_iota(jnp.int32, (rl, nz), 1)
    for a in range(az):
        diffs = [[], [], []]
        sums = []
        for c in range(comp):
            x = adj[c, a]
            f0 = adj[c, a + 1] if a + 1 < az else halo_a[1, c]
            b0 = adj[c, a - 1] if a > 0 else halo_a[0, c]
            f1 = jnp.where(row == rl - 1, halo_r[1, c, a, 0:1, :], pltpu.roll(x, rl - 1, 0))
            b1 = jnp.where(row == 0, halo_r[0, c, a, 7:8, :], pltpu.roll(x, 1, 0))
            f2 = jnp.where(lane == nz - 1, 0.0, pltpu.roll(x, nz - 1, 1))
            b2 = jnp.where(lane == 0, 0.0, pltpu.roll(x, 1, 1))
            diffs[0].append(f0 - b0)
            diffs[1].append(f1 - b1)
            diffs[2].append(f2 - b2)
            sums.append(((f0 + b0) + (f1 + b1)) + (f2 + b2) - 6.0 * x)
        for c in range(comp):
            turned = jnp.zeros((rl, nz), jnp.float32)
            for d in range(3):
                for k in range(comp):
                    turned = turned + jac[0, d, k : k + 1, c : c + 1] * diffs[d][k]
            out_ref[c, a] = adj[c, a] + step[a] * (0.5 * turned + SMOOTHING * sums[c])

    if few:
        for j in range(1, nc):
            tgt_copies[j - 1].wait_recv()
            build_columns(j, j)

    for c in part_copies:
        c.wait_recv()
    total = part[0]
    for k in range(1, no):
        total = total + part[k]
    src[0] = total
    ps_ref[...] = total
    src_copies = [
        remote(src.at[0], src.at[j], s_send.at[j], s_recv.at[j], (peers_c[j], g))
        for j in range(1, nc)
    ]
    for c in src_copies:
        c.start()

    def land(j, slot, first):
        rad = mod(div(tgt[j], nz), radial_all)
        hits = [rad[t : t + 1, :] == row_id for t in range(tiles)]
        for c in range(comp):
            value = src[j, c]
            high = value.astype(jnp.bfloat16).astype(jnp.float32)
            for p, piece in enumerate((high, value - high)):
                top = (p * comp + c) * rl
                for t in range(tiles):
                    a_buf[slot, top : top + rl, t * tile : (t + 1) * tile] = jnp.where(
                        hits[t], piece[t : t + 1, :], 0.0
                    ).astype(jnp.bfloat16)
        got = lax.dot_general(
            a_buf[slot], bt[j if few else 0], NT, preferred_element_type=jnp.float32
        )
        got = got[: comp * rl] + got[comp * rl :]
        if first:
            acc[...] = got
        else:
            acc[...] += got

    if few:
        land(0, 0, True)
        for j in range(1, nc):
            src_copies[j - 1].wait_recv()
            land(j, j % 2, False)
    else:
        build_columns(0, 0)
        land(0, 0, True)

        def one(j, carry):
            remote(tgt.at[0], tgt.at[j], t_send.at[j], t_recv.at[j], (me, g)).wait_recv()
            remote(src.at[0], src.at[j], s_send.at[j], s_recv.at[j], (me, g)).wait_recv()
            build_columns(j, 0)
            land(j, 0, False)
            return carry

        lax.fori_loop(1, nc, one, 0)

    for c in range(comp):
        for a in range(az):
            out_ref[c, a] += acc[c * rl : (c + 1) * rl, a * nz : (a + 1) * nz]

    for c in part_copies + tgt_copies + az_copies + src_copies:
        c.wait_send()

    @pl.when(has_after)
    def _():
        up.wait_send()

    @pl.when(has_before)
    def _():
        down.wait_send()


def on_device(
    nc, no, histories, amplitude, weights, retarded, owner_block, owner_cell, adjoint, step_size, jacobian
):
    tiles = retarded.shape[1]
    tile = weights.shape[0] // tiles
    comp, az, rl, nz = adjoint.shape
    ob = owner_block.reshape(tiles, tile)
    oc = owner_cell.reshape(tiles, tile)
    args = (histories, amplitude, weights, retarded, ob, oc, adjoint, step_size, jacobian)
    slots = nc if nc <= 16 else 1
    f32 = jnp.float32
    dma = pltpu.SemaphoreType.DMA
    out, ps = pl.pallas_call(
        functools.partial(kernel, nc, no),
        out_shape=(
            jax.ShapeDtypeStruct(adjoint.shape, f32),
            jax.ShapeDtypeStruct((comp, tiles, tile), f32),
        ),
        in_specs=[pl.BlockSpec(memory_space=pl.ANY)] * len(args),
        out_specs=(pl.BlockSpec(memory_space=pltpu.VMEM),) * 2,
        scratch_shapes=[pltpu.VMEM(x.shape, x.dtype) for x in args]
        + [
            pltpu.VMEM((no, comp, tiles, tile), f32),
            pltpu.VMEM((nc, comp, tiles, tile), f32),
            pltpu.VMEM((nc, tiles, tile), jnp.int32),
            pltpu.VMEM((2, comp, rl, nz), f32),
            pltpu.VMEM((2, comp, az, 8, nz), f32),
            pltpu.VMEM((2, 2 * comp * rl, tiles * tile), jnp.bfloat16),
            pltpu.VMEM((slots, az * nz, tiles * tile), jnp.bfloat16),
            pltpu.VMEM((comp * rl, az * nz), f32),
            dma((len(args),)),
            dma((no,)),
            dma((no,)),
            dma((nc,)),
            dma((nc,)),
            dma((nc,)),
            dma((nc,)),
            dma((4,)),
            dma((4,)),
        ],
        compiler_params=pltpu.CompilerParams(
            collective_id=0, has_side_effects=True, vmem_limit_bytes=48 * 1024 * 1024
        ),
        name="rotor_step",
    )(*args)
    return out, ps.reshape(comp, tiles * tile)


def solution(mesh):
    return jax.shard_map(
        functools.partial(on_device, mesh.shape["cells"], mesh.shape["obs"]),
        mesh=mesh,
        in_specs=(
            P("obs", None),
            P("obs", None, "cells"),
            P("cells", None),
            P("obs", "cells"),
            P("cells"),
            P("cells"),
            P(None, "cells", "obs", None),
            P("cells", "obs", None),
            P("cells", None, None, None),
        ),
        out_specs=(P(None, "cells", "obs", None), P(None, "cells")),
        check_vma=False,
    )
```

time: 94.1 us -> 21.3 us (0.23)
  other arithmetic: 33.4 us -> 0 us
  blocking collectives: 17.3 us -> 0 us
  starting transfers between devices: 17.1 us -> 0 us
  Pallas kernels: 0 us -> 16.2 us
  local copies, waits for them, and re-layouts: 16.5 us -> 4.16 us
  waiting for transfers between devices: 4.98 us -> 0 us
  matrix products: 2.79 us -> 0 us
    scatter-add x1 -> x0, other arithmetic: 23.2 us -> none  [on_device(): surface = empty_field.at[:, landing].add(received, mode='drop')]
    psum x1 -> x0, blocking collectives: 17.3 us -> none  [on_device(): panel_source = lax.psum(partial_value, 'obs')]
    pallas_call x0 -> x1, Pallas kernels: none -> 16.2 us  [on_device(): pl.pallas_call(functools.partial(kernel, nc, no), out_shape=(jax.ShapeDty...]
    all_to_all x2 -> x0, starting transfers between devices: 8.58 us -> none  [the longest x1 5.2 us: on_device(): lax.all_to_all(out_index, 'cells', split_axis=1, concat_axis=1, tiled=True)]
    ppermute x4 -> x0, starting transfers between devices: 8.52 us -> none  [the longest x2 5.15 us: extended(): lax.ppermute(tail, axis, [(i, (i + 1) % count) for i in range(ends)])]
    all_to_all x2 -> x0, waiting for transfers between devices: 4.97 us -> none  [the longest x1 4.97 us: on_device(): lax.all_to_all(outgoing, 'cells', split_axis=1, concat_axis=1, tiled=True)]
    scatter x1 -> x0, local copies, waits for them, and re-layouts: 3.59 us -> none  [on_device(): jnp.zeros((COMP, devices * capacity), jnp.float32).at[:, slot_of]]
    select_n x8 -> x0, other arithmetic: 3.31 us -> none  [the longest x7 2.85 us: on_device(): shifted = jnp.where(chosen[:, :, None], moved, shifted)]
  transfers between devices with their start and end apart: 6 -> 0, of which waited for: 1 -> 0; matrix products, arithmetic and copies ran while one was open for 43% -> 0% of each run, Pallas kernels for 0% -> 0%
where the time goes in v1:
time: 21.3 us; the launch traced here: 21.1 us
  Pallas kernels  16.2 us (76%)
  local copies, waits for them, and re-layouts  4.16 us (20%)
  between operations  0.73 us (3%)
    pallas_call x1, Pallas kernels, on_device(): pl.pallas_call(functools.partial(kernel, nc, no), out_shape=(jax.ShapeDty...  16.2 us
    unnamed x19, local copies, waits for them, and re-layouts  4.16 us

profile of v1, /device:TPU:0, one launch (start us, length us, event | category | flops | bytes accessed | tf_op | source)
XLA Modules:
  0.0 21.1 jit_solution(13910765057496975548)
XLA Ops:
  0.6 0.0 copy-start.6
  0.6 0.8 %copy.12.ret_h = s32[16,8]{1,0:T(8,128)S(1)} copy(s32[16,8]{0,1:T(8,128)} %param.12) | data formatting | bytes 1024 | tf_op args[3]
  1.4 0.0 copy-done.6
  1.4 0.0 copy-start.1
  1.4 0.0 copy-start.2
  1.4 0.0 copy-start.3
  1.4 0.0 copy-start.4
  1.4 0.0 copy-start.5
  1.5 1.1 %copy.11.amp_h = bf16[16,5,1024]{2,1,0:T(8,128)(2,1)S(1)} copy(bf16[16,5,1024]{2,0,1:T(8,128)(2,1)} %param.10) | data formatting | bytes 327680 | tf_op args[1]
  2.5 0.0 copy-done.1
  2.5 0.0 copy-done.2
  2.5 0.0 copy-done.3
  2.6 0.0 copy-done.4
  2.6 0.0 copy-done.5
  2.6 0.0 copy-start
  2.6 1.0 %copy-done = bf16[1024,256]{1,0:T(8,128)(2,1)S(1)} copy-done((bf16[1024,256]{1,0:T(8,128)(2,1)S(1)}, bf16[1024,256]{1,0:T(8,128)(2,1)}, u32[]{:S(2)}) %copy-start) | copy-done | bytes 524312
  3.6 16.2 %rotor_step.1 = (f32[5,2,16,128]{3,2,1,0:T(8,128)S(1)}, f32[5,8,128]{2,1,0:T(8,128)S(1)}) custom-call(bf16[16,384]{1,0:T(8,128)(2,1)S(1)} %copy-done.3, bf16[16,5,1024]{2,1,0:T(8,128)(2,1)S(1)} %copy.11.amp_h, bf16[1024,256]{1,0:T(8,128)(2,1)S(1)} %copy-done, s32[16,8]{1,0:T(8,128)S(1)} %copy.12.ret_h, s32[8,128]{1,0:T(8,128)S(1)} %bitcast.7, ...), custom_call_target="tpu_custom_call" | custom-call | tf_op jit(solution)/shard_map/rotor_step/pallas_call | solution.py:285
  19.8 0.6 %copy.16 = f32[1,5,8,128]{3,1,2,0:T(8,128)} copy(f32[1,5,8,128]{3,2,1,0:T(8,128)S(1)} %bitcast.6) | data formatting | bytes 40960
  20.5 0.6 %copy.18 = f32[5,2,16,128]{3,2,1,0:T(8,128)} copy(f32[5,2,16,128]{3,2,1,0:T(8,128)S(1)} %get-tuple-element.8) | data formatting | bytes 163840
  (1 shorter events, 0.0 us)
Async XLA Ops:
  0.6 0.8 %copy-start.6 = (f32[1,3,5,5]{3,0,2,1:T(1,128)S(1)}, f32[1,3,5,5]{3,0,2,1:T(1,128)}, u32[]{:S(2)}) copy-start(f32[1,3,5,5]{3,0,2,1:T(1,128)} %param.17) | copy-start | bytes 904
  1.4 1.1 %copy-start.1 = (f32[5,2,16,128]{3,2,1,0:T(8,128)S(1)}, f32[5,2,16,128]{3,2,1,0:T(8,128)}, u32[]{:S(2)}) copy-start(f32[5,2,16,128]{3,2,1,0:T(8,128)} %adj_h.1) | copy-start | bytes 245764
  1.4 1.1 %copy-start.2 = (f32[2,16,128]{2,1,0:T(8,128)S(1)}, f32[2,16,128]{2,1,0:T(8,128)}, u32[]{:S(2)}) copy-start(f32[2,16,128]{2,1,0:T(8,128)} %step_h.1) | copy-start | bytes 49156
  1.4 1.1 %copy-start.3 = (bf16[16,384]{1,0:T(8,128)(2,1)S(1)}, bf16[16,384]{1,0:T(8,128)(2,1)}, u32[]{:S(2)}) copy-start(bf16[16,384]{1,0:T(8,128)(2,1)} %hist_h.1) | copy-start | bytes 36868
  1.4 1.1 %copy-start.4 = (s32[1024]{0:T(1024)S(1)}, s32[1024]{0:T(1024)}, u32[]{:S(2)}) copy-start(s32[1024]{0:T(1024)} %param.13) | copy-start | bytes 12292
  1.4 1.1 %copy-start.5 = (s32[1024]{0:T(1024)S(1)}, s32[1024]{0:T(1024)}, u32[]{:S(2)}) copy-start(s32[1024]{0:T(1024)} %param.14) | copy-start | bytes 12292
  2.6 1.0 %copy-start = (bf16[1024,256]{1,0:T(8,128)(2,1)S(1)}, bf16[1024,256]{1,0:T(8,128)(2,1)}, u32[]{:S(2)}) copy-start(bf16[1024,256]{1,0:T(8,128)(2,1)} %wts_h.1) | copy-start | bytes 1572868

commit v2 on v1

--- a/solution.py
+++ b/solution.py
@@ -60,10 +60,10 @@
     for k in range(1, no):
         pl.semaphore_signal(barrier, inc=1, device_id=(me, peers_o[k]), device_id_type=MESH)
 
-    nobs, comp = amp.shape[0], amp.shape[1]
+    comp, nobs = amp.shape[0], amp.shape[1]
     samples = wts.shape[1]
     hlen = hist.shape[1]
-    tiles = ret.shape[1]
+    tiles = ret.shape[0]
     tile = wts.shape[0] // tiles
     az, rl, nz = adj.shape[1:]
     radial_all = rl * no
@@ -75,11 +75,15 @@
     loads[3].wait()
     tgt[0] = ob[...] * block_cells + oc[...]
     series = hist[...].astype(jnp.float32)
-    offsets = ret[...]
+    same = lax.broadcasted_iota(jnp.int32, (nobs, nobs), 0) == lax.broadcasted_iota(
+        jnp.int32, (nobs, nobs), 1
+    )
+    offsets = ret[...].astype(jnp.float32)
     span = hlen - samples
     windows = []
     for t in range(tiles):
-        off = offsets[:, t : t + 1]
+        off = jnp.sum(jnp.where(same, offsets[t : t + 1, :], 0.0), axis=1, keepdims=True)
+        off = off.astype(jnp.int32)
         x = series
         for bit in reversed(range(span.bit_length())):
             amount = 1 << bit
@@ -91,11 +95,9 @@
     for t in range(tiles):
         cols = slice(t * tile, (t + 1) * tile)
         proj = lax.dot_general(windows[t], wts[cols, :], NT, preferred_element_type=jnp.float32)
-        total = jnp.zeros((comp, tile), jnp.float32)
-        for o in range(nobs):
-            total = total + amp[o, :, cols].astype(jnp.float32) * proj[o : o + 1, :]
         for c in range(comp):
-            part[g, c, t : t + 1, :] = total[c : c + 1, :]
+            product = amp[c, :, cols].astype(jnp.float32) * proj
+            part[g, c, t : t + 1, :] = jnp.sum(product, axis=0, keepdims=True)
     loads[6].wait()
     loads[7].wait()
     loads[8].wait()
@@ -193,7 +195,7 @@
             turned = jnp.zeros((rl, nz), jnp.float32)
             for d in range(3):
                 for k in range(comp):
-                    turned = turned + jac[0, d, k : k + 1, c : c + 1] * diffs[d][k]
+                    turned = turned + jac[d, k, :, c : c + 1] * diffs[d][k]
             out_ref[c, a] = adj[c, a] + step[a] * (0.5 * turned + SMOOTHING * sums[c])
 
     if few:
@@ -278,7 +280,17 @@
     comp, az, rl, nz = adjoint.shape
     ob = owner_block.reshape(tiles, tile)
     oc = owner_cell.reshape(tiles, tile)
-    args = (histories, amplitude, weights, retarded, ob, oc, adjoint, step_size, jacobian)
+    args = (
+        histories,
+        jnp.transpose(amplitude, (1, 0, 2)),
+        weights,
+        retarded.T,
+        ob,
+        oc,
+        adjoint,
+        step_size,
+        jnp.transpose(jacobian, (1, 2, 0, 3)),
+    )
     slots = nc if nc <= 16 else 1
     f32 = jnp.float32
     dma = pltpu.SemaphoreType.DMA
@@ -288,7 +300,7 @@
             jax.ShapeDtypeStruct(adjoint.shape, f32),
             jax.ShapeDtypeStruct((comp, tiles, tile), f32),
         ),
-        in_specs=[pl.BlockSpec(memory_space=pl.ANY)] * len(args),
+        in_specs=[pl.BlockSpec(memory_space=pltpu.HBM)] * len(args),
         out_specs=(pl.BlockSpec(memory_space=pltpu.VMEM),) * 2,
         scratch_shapes=[pltpu.VMEM(x.shape, x.dtype) for x in args]
         + [
@@ -311,7 +323,7 @@
             dma((4,)),
         ],
         compiler_params=pltpu.CompilerParams(
-            collective_id=0, has_side_effects=True, vmem_limit_bytes=48 * 1024 * 1024
+            collective_id=0, has_side_effects=True, vmem_limit_bytes=67_043_328
         ),
         name="rotor_step",
     )(*args)

time: 21.3 us -> 20.3 us (0.953)
  local copies, waits for them, and re-layouts: 4.16 us -> 2.88 us
  Pallas kernels: 16.2 us -> 16.5 us
    unnamed x19 -> x2, local copies, waits for them, and re-layouts: 4.16 us -> 2.88 us
    pallas_call x1, Pallas kernels: 16.2 us -> 16.5 us  [on_device(): pl.pallas_call(functools.partial(kernel, nc, no), out_shape=(jax.ShapeDty...]
where the time goes in v2:
time: 20.3 us; the launch traced here: 20.1 us
  Pallas kernels  16.5 us (81%)
  local copies, waits for them, and re-layouts  2.88 us (14%)
  between operations  0.64 us (3%)
    pallas_call x1, Pallas kernels, on_device(): pl.pallas_call(functools.partial(kernel, nc, no), out_shape=(jax.ShapeDty...  16.5 us
    unnamed x2, local copies, waits for them, and re-layouts  2.88 us

profile of v2, /device:TPU:0, one launch (start us, length us, event | category | flops | bytes accessed | tf_op | source)
XLA Modules:
  0.0 20.1 jit_solution(12899493352932685118)
XLA Ops:
  0.6 16.5 %rotor_step.1 = (f32[5,2,16,128]{3,2,1,0:T(8,128)}, f32[5,8,128]{2,1,0:T(8,128)}) custom-call(bf16[16,384]{1,0:T(8,128)(2,1)} %hist_h.1, bf16[5,16,1024]{2,1,0:T(8,128)(2,1)} %bitcast.9, bf16[1024,256]{1,0:T(8,128)(2,1)} %wts_h.1, s32[8,16]{1,0:T(8,128)} %bitcast.13, s32[8,128]{1,0:T(8,128)} %bitcast.14, s32[8,128]{1,0:T(8,128)} %bitcast.15, ...), custom_call_target="tpu_custom_call" | custom-call | tf_op jit(solution)/shard_map/rotor_step/pallas_call | solution.py:297
  17.2 1.4 %copy.13 = f32[1,5,8,128]{3,1,2,0:T(8,128)} copy(f32[1,5,8,128]{3,2,1,0:T(8,128)} %bitcast.11) | data formatting | bytes 40960
  18.5 1.5 %copy.15 = f32[5,2,16,128]{3,2,1,0:T(8,128)} copy(f32[5,2,16,128]{3,2,1,0:T(8,128)} %get-tuple-element.8) | data formatting | bytes 163840

commit v3 on v2

--- a/solution.py
+++ b/solution.py
@@ -39,7 +39,7 @@
     hist_h, amp_h, wts_h, ret_h, ob_h, oc_h, adj_h, step_h, jac_h,
     out_ref, ps_ref,
     hist, amp, wts, ret, ob, oc, adj, step, jac,
-    part, src, tgt, halo_a, halo_r, a_buf, bt, acc,
+    part, src, tgt, halo_a, halo_r, edge, a_buf, bt, acc,
     in_sem, ps_send, ps_recv, s_send, s_recv, t_send, t_recv, h_send, h_recv,
 ):
     me, g = lax.axis_index("cells"), lax.axis_index("obs")
@@ -90,6 +90,12 @@
             moved = pltpu.roll(x, hlen - amount, 1)
             x = jnp.where((off >> bit & 1) == 1, moved, x)
         windows.append(x[:, :samples].astype(jnp.bfloat16))
+    loads[6].wait()
+    for c in range(comp):
+        for a in range(az):
+            i = c * az + a
+            edge[0, i : i + 1, :] = adj[c, a, rl - 1 : rl, :]
+            edge[1, i : i + 1, :] = adj[c, a, 0:1, :]
     loads[4].wait()
     loads[5].wait()
     for t in range(tiles):
@@ -98,10 +104,6 @@
         for c in range(comp):
             product = amp[c, :, cols].astype(jnp.float32) * proj
             part[g, c, t : t + 1, :] = jnp.sum(product, axis=0, keepdims=True)
-    loads[6].wait()
-    loads[7].wait()
-    loads[8].wait()
-
     pl.semaphore_wait(barrier, nc - 1 + no - 1)
 
     def remote(s, d, ss, rs, dev):
@@ -129,8 +131,8 @@
     for c in az_copies:
         c.start()
     g_after, g_before = lax.rem(g + 1, no), lax.rem(g + no - 1, no)
-    up = remote(adj.at[:, :, pl.ds(rl - 8, 8)], halo_r.at[0], h_send.at[2], h_recv.at[2], (me, g_after))
-    down = remote(adj.at[:, :, pl.ds(0, 8)], halo_r.at[1], h_send.at[3], h_recv.at[3], (me, g_before))
+    up = remote(edge.at[0], halo_r.at[0], h_send.at[2], h_recv.at[2], (me, g_after))
+    down = remote(edge.at[1], halo_r.at[1], h_send.at[3], h_recv.at[3], (me, g_before))
     has_after, has_before = g < no - 1, g > 0
 
     @pl.when(has_after)
@@ -154,49 +156,6 @@
     few = bt.shape[0] == nc
     if few:
         build_columns(0, 0)
-
-    for c in az_copies:
-        c.wait_recv()
-
-    @pl.when(has_before)
-    def _():
-        up.wait_recv()
-
-    @pl.when(has_after)
-    def _():
-        down.wait_recv()
-
-    @pl.when(jnp.logical_not(has_before))
-    def _():
-        halo_r[0] = jnp.zeros(halo_r.shape[1:], jnp.float32)
-
-    @pl.when(jnp.logical_not(has_after))
-    def _():
-        halo_r[1] = jnp.zeros(halo_r.shape[1:], jnp.float32)
-
-    row = lax.broadcasted_iota(jnp.int32, (rl, nz), 0)
-    lane = lax.broadcasted_iota(jnp.int32, (rl, nz), 1)
-    for a in range(az):
-        diffs = [[], [], []]
-        sums = []
-        for c in range(comp):
-            x = adj[c, a]
-            f0 = adj[c, a + 1] if a + 1 < az else halo_a[1, c]
-            b0 = adj[c, a - 1] if a > 0 else halo_a[0, c]
-            f1 = jnp.where(row == rl - 1, halo_r[1, c, a, 0:1, :], pltpu.roll(x, rl - 1, 0))
-            b1 = jnp.where(row == 0, halo_r[0, c, a, 7:8, :], pltpu.roll(x, 1, 0))
-            f2 = jnp.where(lane == nz - 1, 0.0, pltpu.roll(x, nz - 1, 1))
-            b2 = jnp.where(lane == 0, 0.0, pltpu.roll(x, 1, 1))
-            diffs[0].append(f0 - b0)
-            diffs[1].append(f1 - b1)
-            diffs[2].append(f2 - b2)
-            sums.append(((f0 + b0) + (f1 + b1)) + (f2 + b2) - 6.0 * x)
-        for c in range(comp):
-            turned = jnp.zeros((rl, nz), jnp.float32)
-            for d in range(3):
-                for k in range(comp):
-                    turned = turned + jac[d, k, :, c : c + 1] * diffs[d][k]
-            out_ref[c, a] = adj[c, a] + step[a] * (0.5 * turned + SMOOTHING * sums[c])
 
     if few:
         for j in range(1, nc):
@@ -237,6 +196,51 @@
             acc[...] = got
         else:
             acc[...] += got
+
+    loads[7].wait()
+    loads[8].wait()
+    for c in az_copies:
+        c.wait_recv()
+
+    @pl.when(has_before)
+    def _():
+        up.wait_recv()
+
+    @pl.when(has_after)
+    def _():
+        down.wait_recv()
+
+    @pl.when(jnp.logical_not(has_before))
+    def _():
+        halo_r[0] = jnp.zeros(halo_r.shape[1:], jnp.float32)
+
+    @pl.when(jnp.logical_not(has_after))
+    def _():
+        halo_r[1] = jnp.zeros(halo_r.shape[1:], jnp.float32)
+
+    row = lax.broadcasted_iota(jnp.int32, (rl, nz), 0)
+    lane = lax.broadcasted_iota(jnp.int32, (rl, nz), 1)
+    for a in range(az):
+        diffs = [[], [], []]
+        sums = []
+        for c in range(comp):
+            x = adj[c, a]
+            f0 = adj[c, a + 1] if a + 1 < az else halo_a[1, c]
+            b0 = adj[c, a - 1] if a > 0 else halo_a[0, c]
+            f1 = jnp.where(row == rl - 1, halo_r[1, c * az + a : c * az + a + 1, :], pltpu.roll(x, rl - 1, 0))
+            b1 = jnp.where(row == 0, halo_r[0, c * az + a : c * az + a + 1, :], pltpu.roll(x, 1, 0))
+            f2 = jnp.where(lane == nz - 1, 0.0, pltpu.roll(x, nz - 1, 1))
+            b2 = jnp.where(lane == 0, 0.0, pltpu.roll(x, 1, 1))
+            diffs[0].append(f0 - b0)
+            diffs[1].append(f1 - b1)
+            diffs[2].append(f2 - b2)
+            sums.append(((f0 + b0) + (f1 + b1)) + (f2 + b2) - 6.0 * x)
+        for c in range(comp):
+            turned = jnp.zeros((rl, nz), jnp.float32)
+            for d in range(3):
+                for k in range(comp):
+                    turned = turned + jac[d, k, :, c : c + 1] * diffs[d][k]
+            out_ref[c, a] = adj[c, a] + step[a] * (0.5 * turned + SMOOTHING * sums[c])
 
     if few:
         land(0, 0, True)
@@ -297,8 +301,8 @@
     out, ps = pl.pallas_call(
         functools.partial(kernel, nc, no),
         out_shape=(
-            jax.ShapeDtypeStruct(adjoint.shape, f32),
-            jax.ShapeDtypeStruct((comp, tiles, tile), f32),
+            pltpu.VMEM(adjoint.shape, f32),
+            pltpu.VMEM((comp, tiles, tile), f32),
         ),
         in_specs=[pl.BlockSpec(memory_space=pltpu.HBM)] * len(args),
         out_specs=(pl.BlockSpec(memory_space=pltpu.VMEM),) * 2,
@@ -308,7 +312,8 @@
             pltpu.VMEM((nc, comp, tiles, tile), f32),
             pltpu.VMEM((nc, tiles, tile), jnp.int32),
             pltpu.VMEM((2, comp, rl, nz), f32),
-            pltpu.VMEM((2, comp, az, 8, nz), f32),
+            pltpu.VMEM((2, comp * az, nz), f32),
+            pltpu.VMEM((2, comp * az, nz), f32),
             pltpu.VMEM((2, 2 * comp * rl, tiles * tile), jnp.bfloat16),
             pltpu.VMEM((slots, az * nz, tiles * tile), jnp.bfloat16),
             pltpu.VMEM((comp * rl, az * nz), f32),
@@ -323,7 +328,7 @@
             dma((4,)),
         ],
         compiler_params=pltpu.CompilerParams(
-            collective_id=0, has_side_effects=True, vmem_limit_bytes=67_043_328
+            collective_id=0, has_side_effects=True, vmem_limit_bytes=67_043_328 - 120_000
         ),
         name="rotor_step",
     )(*args)

time: 20.3 us -> 17.2 us (0.85)
  local copies, waits for them, and re-layouts: 2.88 us -> 1.26 us
  Pallas kernels: 16.5 us -> 15.1 us
    unnamed x2, local copies, waits for them, and re-layouts: 2.88 us -> 1.26 us
    pallas_call x1, Pallas kernels: 16.5 us -> 15.1 us  [on_device(): pl.pallas_call(functools.partial(kernel, nc, no), out_shape=(pltpu.VMEM(a...]
where the time goes in v3:
time: 17.2 us; the launch traced here: 17 us
  Pallas kernels  15.1 us (88%)
  local copies, waits for them, and re-layouts  1.26 us (7%)
  between operations  0.64 us (4%)
    pallas_call x1, Pallas kernels, on_device(): pl.pallas_call(functools.partial(kernel, nc, no), out_shape=(pltpu.VMEM(a...  15.1 us
    unnamed x2, local copies, waits for them, and re-layouts  1.26 us

profile of v3, /device:TPU:0, one launch (start us, length us, event | category | flops | bytes accessed | tf_op | source)
XLA Modules:
  0.0 17.0 jit_solution(6677809870896207449)
XLA Ops:
  0.6 15.1 %rotor_step.1 = (f32[5,2,16,128]{3,2,1,0:T(8,128)S(1)}, f32[5,8,128]{2,1,0:T(8,128)S(1)}) custom-call(bf16[16,384]{1,0:T(8,128)(2,1)} %hist_h.1, bf16[5,16,1024]{2,1,0:T(8,128)(2,1)} %bitcast.10, bf16[1024,256]{1,0:T(8,128)(2,1)} %wts_h.1, s32[8,16]{1,0:T(8,128)} %bitcast.13, s32[8,128]{1,0:T(8,128)} %bitcast.14, s32[8,128]{1,0:T(8,128)} %bitcast.15, ...), custom_call_target="tpu_custom_call" | custom-call | tf_op jit(solution)/shard_map/rotor_step/pallas_call | solution.py:301
  15.7 0.6 %copy.15 = f32[5,2,16,128]{3,2,1,0:T(8,128)} copy(f32[5,2,16,128]{3,2,1,0:T(8,128)S(1)} %get-tuple-element.6) | data formatting | bytes 163840
  16.3 0.6 %copy.13 = f32[1,5,8,128]{3,1,2,0:T(8,128)} copy(f32[1,5,8,128]{3,2,1,0:T(8,128)S(1)} %bitcast.9) | data formatting | bytes 40960

commit v4 on v3

--- a/solution.py
+++ b/solution.py
@@ -104,45 +104,6 @@
         for c in range(comp):
             product = amp[c, :, cols].astype(jnp.float32) * proj
             part[g, c, t : t + 1, :] = jnp.sum(product, axis=0, keepdims=True)
-    pl.semaphore_wait(barrier, nc - 1 + no - 1)
-
-    def remote(s, d, ss, rs, dev):
-        return pltpu.make_async_remote_copy(
-            src_ref=s, dst_ref=d, send_sem=ss, recv_sem=rs, device_id=dev, device_id_type=MESH
-        )
-
-    part_copies = [
-        remote(part.at[g], part.at[g], ps_send.at[k], ps_recv.at[k], (me, peers_o[k]))
-        for k in range(1, no)
-    ]
-    for c in part_copies:
-        c.start()
-    tgt_copies = [
-        remote(tgt.at[0], tgt.at[j], t_send.at[j], t_recv.at[j], (peers_c[j], g))
-        for j in range(1, nc)
-    ]
-    for c in tgt_copies:
-        c.start()
-    after, before = lax.rem(me + 1, nc), lax.rem(me + nc - 1, nc)
-    az_copies = [
-        remote(adj.at[:, az - 1], halo_a.at[0], h_send.at[0], h_recv.at[0], (after, g)),
-        remote(adj.at[:, 0], halo_a.at[1], h_send.at[1], h_recv.at[1], (before, g)),
-    ]
-    for c in az_copies:
-        c.start()
-    g_after, g_before = lax.rem(g + 1, no), lax.rem(g + no - 1, no)
-    up = remote(edge.at[0], halo_r.at[0], h_send.at[2], h_recv.at[2], (me, g_after))
-    down = remote(edge.at[1], halo_r.at[1], h_send.at[3], h_recv.at[3], (me, g_before))
-    has_after, has_before = g < no - 1, g > 0
-
-    @pl.when(has_after)
-    def _():
-        up.start()
-
-    @pl.when(has_before)
-    def _():
-        down.start()
-
     column_id = lax.broadcasted_iota(jnp.int32, (az * nz, tile), 0) + me * (az * nz)
     row_id = lax.broadcasted_iota(jnp.int32, (rl, tile), 0) + g * rl
 
@@ -157,8 +118,47 @@
     if few:
         build_columns(0, 0)
 
+    pl.semaphore_wait(barrier, nc - 1 + no - 1)
+
+    def remote(s, d, ss, rs, dev):
+        return pltpu.make_async_remote_copy(
+            src_ref=s, dst_ref=d, send_sem=ss, recv_sem=rs, device_id=dev, device_id_type=MESH
+        )
+
+    part_copies = [
+        remote(part.at[g], part.at[g], ps_send.at[k], ps_recv.at[k], (me, peers_o[k]))
+        for k in range(1, no)
+    ]
+    for c in part_copies:
+        c.start()
+    tgt_copies = [
+        remote(tgt.at[0], tgt.at[j], t_send.at[j], t_recv.at[j], (peers_c[j], g))
+        for j in range(1, nc)
+    ]
+    for c in tgt_copies:
+        c.start()
+    after, before = lax.rem(me + 1, nc), lax.rem(me + nc - 1, nc)
+    az_copies = [
+        remote(adj.at[:, az - 1], halo_a.at[0], h_send.at[0], h_recv.at[0], (after, g)),
+        remote(adj.at[:, 0], halo_a.at[1], h_send.at[1], h_recv.at[1], (before, g)),
+    ]
+    for c in az_copies:
+        c.start()
+    g_after, g_before = lax.rem(g + 1, no), lax.rem(g + no - 1, no)
+    up = remote(edge.at[0], halo_r.at[0], h_send.at[2], h_recv.at[2], (me, g_after))
+    down = remote(edge.at[1], halo_r.at[1], h_send.at[3], h_recv.at[3], (me, g_before))
+    has_after, has_before = g < no - 1, g > 0
+
+    @pl.when(has_after)
+    def _():
+        up.start()
+
+    @pl.when(has_before)
+    def _():
+        down.start()
+
     if few:
-        for j in range(1, nc):
+        for j in range(1, nc // 2):
             tgt_copies[j - 1].wait_recv()
             build_columns(j, j)
 
@@ -245,6 +245,10 @@
     if few:
         land(0, 0, True)
         for j in range(1, nc):
+            if j == 1:
+                for i in range(nc // 2, nc):
+                    tgt_copies[i - 1].wait_recv()
+                    build_columns(i, i)
             src_copies[j - 1].wait_recv()
             land(j, j % 2, False)
     else:

time: 17.2 us -> 16.8 us (0.977)
  Pallas kernels: 15.1 us -> 14.7 us
    pallas_call x1, Pallas kernels: 15.1 us -> 14.7 us  [on_device(): pl.pallas_call(functools.partial(kernel, nc, no), out_shape=(pltpu.VMEM(a...]
where the time goes in v4:
time: 16.8 us; the launch traced here: 16.6 us
  Pallas kernels  14.7 us (88%)
  local copies, waits for them, and re-layouts  1.26 us (8%)
  between operations  0.64 us (4%)
    pallas_call x1, Pallas kernels, on_device(): pl.pallas_call(functools.partial(kernel, nc, no), out_shape=(pltpu.VMEM(a...  14.7 us
    unnamed x2, local copies, waits for them, and re-layouts  1.26 us

profile of v4, /device:TPU:0, one launch (start us, length us, event | category | flops | bytes accessed | tf_op | source)
XLA Modules:
  0.0 16.6 jit_solution(17782559376965771911)
XLA Ops:
  0.6 14.7 %rotor_step.1 = (f32[5,2,16,128]{3,2,1,0:T(8,128)S(1)}, f32[5,8,128]{2,1,0:T(8,128)S(1)}) custom-call(bf16[16,384]{1,0:T(8,128)(2,1)} %hist_h.1, bf16[5,16,1024]{2,1,0:T(8,128)(2,1)} %bitcast.10, bf16[1024,256]{1,0:T(8,128)(2,1)} %wts_h.1, s32[8,16]{1,0:T(8,128)} %bitcast.13, s32[8,128]{1,0:T(8,128)} %bitcast.14, s32[8,128]{1,0:T(8,128)} %bitcast.15, ...), custom_call_target="tpu_custom_call" | custom-call | tf_op jit(solution)/shard_map/rotor_step/pallas_call | solution.py:305
  15.3 0.6 %copy.15 = f32[5,2,16,128]{3,2,1,0:T(8,128)} copy(f32[5,2,16,128]{3,2,1,0:T(8,128)S(1)} %get-tuple-element.6) | data formatting | bytes 163840
  15.9 0.6 %copy.13 = f32[1,5,8,128]{3,1,2,0:T(8,128)} copy(f32[1,5,8,128]{3,2,1,0:T(8,128)S(1)} %bitcast.9) | data formatting | bytes 40960
